TPU v7x, 32 devices: a whole 2x2x4 slice. The times are simulated.
32 devices in a mesh: dp: 8 (over y, x, core), mp: 4 (over z).
Axes of the slice: x: 2, y: 2, z: 4, core: 2. Of those that a mesh axis runs over, the one named last changes fastest.
Arguments:
- factor_rows: bfloat16 [4, 8, 8, 768], P('mp', None, 'dp')
- old_statistic: float32 [8, 4, 768, 768], P('dp', 'mp'), may hold values from -1 to 2, as said below
- assignment: int32 [4, 8], P('mp'), may hold values from 0 to 7, each once within a row
- gradient: bfloat16 [8, 4, 768, 512], P('dp', None, None, 'mp'), may hold values from -3 to 3
Outputs:
- update: bfloat16 [8, 4, 768, 512], P('dp', None, None, 'mp')
Inputs may be any that keep to these rules, and one draw needn't show every extreme that they name: Each row of assignment names every block number once. `old_statistic`: each block is symmetric positive definite.
All inputs are finite; a program needn't handle non-finite values.
Results may differ from a plain program's by a relative error of at most 0.001.
The roundings to bfloat16 on the way count: a program that leaves them out, or rounds other values in their place, can miss the bound.
Values may be sent and summed in bfloat16 or wider, within the bound.
No kernel may reach another device: no remote copies, remote signals or barrier semaphores. Data moves between devices by JAX's collectives and lax.ppermute only.
A program may use at most 64 MiB of HBM per device.

v0:
```python
import jax
import jax.numpy as jnp
from jax import lax
from jax.sharding import PartitionSpec as P


def newton_factors(statistic):
    identity = jnp.eye(statistic.shape[0], dtype=jnp.float32)
    frob_norm = jnp.sqrt(jnp.sum(statistic * statistic) + 1e-06)
    normed = statistic / frob_norm
    step_one = ((5.0 * identity - normed) * 0.25).astype(jnp.bfloat16)
    square_one = jnp.dot(step_one, step_one, preferred_element_type=jnp.float32).astype(
        jnp.bfloat16
    )
    product_one = jnp.dot(
        square_one, normed.astype(jnp.bfloat16), preferred_element_type=jnp.float32
    ).astype(jnp.bfloat16)
    coupled_one = jnp.dot(square_one, product_one, preferred_element_type=jnp.float32)
    step_two = ((5.0 * identity - coupled_one) * 0.25).astype(jnp.bfloat16)
    square_two = jnp.dot(step_two, step_two, preferred_element_type=jnp.float32).astype(
        jnp.bfloat16
    )
    product_two = jnp.dot(
        square_two, coupled_one.astype(jnp.bfloat16), preferred_element_type=jnp.float32
    ).astype(jnp.bfloat16)
    coupled_two = jnp.dot(square_two, product_two, preferred_element_type=jnp.float32)
    step_three = ((5.0 * identity - coupled_two) / (4.0 * jnp.sqrt(jnp.sqrt(frob_norm)))).astype(
        jnp.bfloat16
    )
    return jnp.stack([step_one, step_two, step_three])


def body(factor_rows, old_statistic, assignment, gradient):
    chosen = assignment[0]
    picked = jnp.take(factor_rows[0], chosen, axis=0)
    arrived = lax.all_to_all(picked, "dp", split_axis=0, concat_axis=1, tiled=True)
    factors = arrived[0]
    count = factors.shape[0]
    gram = lax.dot_general(
        factors, factors, (((0,), (0,)), ((), ())), preferred_element_type=jnp.float32
    )
    statistic = old_statistic[0, 0] + gram / count
    stacked = newton_factors(statistic)
    first_pass = jnp.einsum(
        "ij,nkjc->nkic",
        stacked[2],
        lax.all_to_all(gradient, "mp", split_axis=1, concat_axis=3, tiled=True),
        preferred_element_type=jnp.float32,
    ).astype(jnp.bfloat16)
    second_pass = jnp.einsum(
        "ij,nkjc->nkic", stacked[1], first_pass, preferred_element_type=jnp.float32
    ).astype(jnp.bfloat16)
    result = jnp.einsum(
        "ij,nkjc->nkic", stacked[0], second_pass, preferred_element_type=jnp.float32
    ).astype(jnp.bfloat16)
    return lax.all_to_all(result, "mp", split_axis=3, concat_axis=1, tiled=True)


def solution(mesh):
    return jax.shard_map(
        body,
        mesh=mesh,
        in_specs=(
            P("mp", None, "dp", None),
            P("dp", "mp", None, None),
            P("mp", None),
            P("dp", None, None, "mp"),
        ),
        out_specs=P("dp", None, None, "mp"),
        check_vma=False,
    )
```

profile of v0, /device:TPU:0, one launch (start us, length us, event | category | flops | bytes accessed | tf_op | source)
XLA Modules:
  0.0 77.3 jit_solution(11541387428655440850)
XLA Ops:
  0.0 0.0 copy-start
  0.0 0.7 fusion.18
  0.7 0.7 compare_and_fusion
  1.3 0.0 copy-done
  1.4 0.6 gather_fusion
  1.9 0.1 bitcast_select_fusion
  2.0 0.5 broadcast.94
  2.5 0.6 reduce
  3.2 0.6 reshape.92
  3.8 5.2 %all-to-all-start = ((bf16[8,2,384]{2,1,0:T(2,128)(2,1)}), bf16[8,2,384]{2,1,0:T(2,128)(2,1)S(1)}, u32[]{:S(2)}, u32[]{:S(2)}) async-start(bf16[8,2,384]{2,1,0:T(2,128)(2,1)} %reshape.92), calls=%async_computation | async-start | bytes 24576 | tf_op jit(solution)/shard_map/all_to_all | solution.py:36
  9.0 2.3 %copy.13 = bf16[1,4,768,128]{2,3,0,1:T(8,128)(2,1)} copy(bf16[1,4,768,128]{3,2,1,0:T(8,128)(2,1)} %param.7) | data formatting | bytes 1572864 | tf_op args[3]
  11.3 2.4 %all-to-all-done = bf16[8,2,384]{2,1,0:T(2,128)(2,1)S(1)} async-done(((bf16[8,2,384]{2,1,0:T(2,128)(2,1)}), bf16[8,2,384]{2,1,0:T(2,128)(2,1)S(1)}, u32[]{:S(2)}, u32[]{:S(2)}) %all-to-all-start) | async-done | bytes 12320 | tf_op jit(solution)/shard_map/all_to_all | solution.py:36
  13.7 4.9 %all-to-all-start.1 = ((bf16[1,4,768,128]{2,3,0,1:T(8,128)(2,1)}), bf16[1,4,768,128]{2,3,0,1:T(8,128)(2,1)}, u32[]{:S(2)}, u32[]{:S(2)}) async-start(bf16[1,4,768,128]{2,3,0,1:T(8,128)(2,1)} %copy.13), calls=%async_computation.1 | async-start | bytes 1572864 | tf_op jit(solution)/shard_map/all_to_all | solution.py:47
  18.6 3.2 %multiply_reduce_fusion = (f32[]{:T(128)}, f32[768,768]{1,0:T(8,128)S(1)}) fusion(bf16[8,1,768]{2,1,0:T(2,128)(2,1)S(1)} %reshape.93, f32[1,1,768,768]{3,2,1,0:T(8,128)} %param.5), kind=kOutput, calls=%fused_computation.11 | convolution fusion | flops 11796479 | bytes 4730884 | tf_op jit(solution)/shard_map/dot_general | solution.py:39
  22.5 0.3 fusion.1
  22.9 2.1 %convolution_convert_fusion.3 = bf16[768,768]{1,0:T(8,128)(2,1)} fusion(bf16[768,768]{1,0:T(8,128)(2,1)S(1)} %fusion.1), kind=kOutput, calls=%fused_computation.16 | convolution fusion | flops 906559488 | bytes 2359296 | tf_op jit(solution)/shard_map/dot_general | solution.py:12
  25.0 5.1 %fusion.11 = f32[768,768]{1,0:T(8,128)} fusion(bf16[768,768]{1,0:T(8,128)(2,1)} %convolution_convert_fusion.3, f32[768,768]{1,0:T(8,128)S(1)} %get-tuple-element.6, f32[]{:T(128)S(6)} %sqrt.9), kind=kOutput, calls=%fused_computation.25 | convolution fusion | flops 1813708800 | bytes 5898244 | tf_op jit(solution)/shard_map/dot_general | solution.py:18
  30.1 0.0 copy-start.1
  30.1 3.6 %convolution_convert_fusion.1 = bf16[768,768]{1,0:T(8,128)(2,1)S(1)} fusion(f32[768,768]{1,0:T(8,128)} %fusion.11), kind=kOutput, calls=%fused_computation.14 | convolution fusion | flops 909508608 | bytes 3538944 | tf_op jit(solution)/shard_map/dot_general | solution.py:20
  33.7 0.0 copy-done.1
  33.8 1.1 %convolution_convert_fusion = bf16[768,768]{1,0:T(8,128)(2,1)S(1)} fusion(bf16[768,768]{1,0:T(8,128)(2,1)S(1)} %convolution_convert_fusion.1, f32[768,768]{1,0:T(8,128)S(1)} %copy-done.1), kind=kOutput, calls=%fused_computation.13 | convolution fusion | flops 907149312 | bytes 4718592 | tf_op jit(solution)/shard_map/dot_general | solution.py:23
  34.9 3.9 %all-to-all-done.1 = bf16[1,4,768,128]{2,3,0,1:T(8,128)(2,1)} async-done(((bf16[1,4,768,128]{2,3,0,1:T(8,128)(2,1)}), bf16[1,4,768,128]{2,3,0,1:T(8,128)(2,1)}, u32[]{:S(2)}, u32[]{:S(2)}) %all-to-all-start.1) | async-done | bytes 786464 | tf_op jit(solution)/shard_map/all_to_all | solution.py:47
  38.7 3.7 %convolution_convert_fusion.6 = bf16[768,512]{1,0:T(8,128)(2,1)} fusion(bf16[768,512]{0,1:T(8,128)(2,1)} %bitcast.8, bf16[768,768]{1,0:T(8,128)(2,1)S(1)} %convolution_convert_fusion.1, bf16[768,768]{1,0:T(8,128)(2,1)S(1)} %convolution_convert_fusion, f32[]{:T(128)S(6)} %mul_shard_map.3), kind=kOutput, calls=%fused_computation.19 | convolution fusion | flops 1513291776 | bytes 3932164 | tf_op jit(solution)/shard_map/ij,nkjc->nkic/dot_general | solution.py:44
  42.5 3.5 %fusion.7 = bf16[1,1,768,512]{2,3,1,0:T(8,128)(2,1)S(1)} fusion(bf16[768,768]{1,0:T(8,128)(2,1)S(1)} %fusion.1, bf16[768,512]{1,0:T(8,128)(2,1)} %convolution_convert_fusion.6, f32[768,768]{1,0:T(8,128)} %fusion.11), kind=kOutput, calls=%fused_computation.21 | convolution fusion | flops 1211695104 | bytes 5111808 | tf_op jit(solution)/shard_map/ij,nkjc->nkic/dot_general | solution.py:53
  45.9 1.2 %copy.25 = bf16[1,1,768,512]{2,1,0,3:T(2,128)(2,1)S(1)} copy(bf16[1,1,768,512]{2,3,1,0:T(8,128)(2,1)S(1)} %fusion.7) | data formatting | bytes 1572864 | tf_op jit(solution)/shard_map/convert_element_type | solution.py:55
  47.1 5.8 %reduce.1 = bf16[512,768]{1,0:T(8,128)(2,1)S(1)} reduce(bf16[512,1,1,768]{3,2,1,0:T(2,128)(2,1)S(1)} %bitcast.60, bf16[]{:T(256)} %broadcast.94), dimensions={1,2}, to_apply=%bitcast.58.reduce_sub_computation | reduce | bytes 1572866
  52.9 0.2 reshape.94
  53.1 22.1 %all_to_all.42 = bf16[4,2,49152]{2,1,0:T(2,128)(2,1)S(1)} all-to-all(bf16[4,2,49152]{2,1,0:T(2,128)(2,1)S(1)} %reshape.94), channel_id=1, replica_groups=mesh['dp'=8,'mp'=4] {'mp'}, dimensions={0} | all-to-all | bytes 1572864 | tf_op jit(solution)/shard_map/all_to_all | solution.py:56
  75.2 0.7 reshape.95
  76.0 0.1 copy.17
  76.1 1.2 %copy.15 = bf16[1,4,768,128]{3,2,1,0:T(8,128)(2,1)} copy(bf16[1,4,768,128]{2,3,1,0:T(8,128)(2,1)S(1)} %bitcast.62) | data formatting | bytes 1572864 | tf_op jit(solution)/shard_map/all_to_all | solution.py:56
  (2 shorter events, 0.0 us)
Async XLA Ops:
  0.0 1.3 %copy-start = (bf16[1,8,1,768]{3,1,2,0:T(8,128)(2,1)S(1)}, bf16[1,8,1,768]{3,1,2,0:T(8,128)(2,1)}, u32[]{:S(2)}) copy-start(bf16[1,8,1,768]{3,1,2,0:T(8,128)(2,1)} %param.4) | copy-start | bytes 36868
  3.8 9.9 %all-to-all-start = ((bf16[8,2,384]{2,1,0:T(2,128)(2,1)}), bf16[8,2,384]{2,1,0:T(2,128)(2,1)S(1)}, u32[]{:S(2)}, u32[]{:S(2)}) async-start(bf16[8,2,384]{2,1,0:T(2,128)(2,1)} %reshape.92), calls=%async_computation | async-start | bytes 24576 | tf_op jit(solution)/shard_map/all_to_all | solution.py:36
  13.7 25.0 %all-to-all-start.1 = ((bf16[1,4,768,128]{2,3,0,1:T(8,128)(2,1)}), bf16[1,4,768,128]{2,3,0,1:T(8,128)(2,1)}, u32[]{:S(2)}, u32[]{:S(2)}) async-start(bf16[1,4,768,128]{2,3,0,1:T(8,128)(2,1)} %copy.13), calls=%async_computation.1 | async-start | bytes 1572864 | tf_op jit(solution)/shard_map/all_to_all | solution.py:47
  30.1 3.7 %copy-start.1 = (f32[768,768]{1,0:T(8,128)S(1)}, f32[768,768]{1,0:T(8,128)}, u32[]{:S(2)}) copy-start(f32[768,768]{1,0:T(8,128)} %fusion.11) | copy-start | bytes 7077892
where the time goes:
time: 77.8 us; the launch traced here: 77.3 us
  matrix products  22.3 us (29%)
  blocking collectives  22.1 us (28%)
  starting transfers between devices  10.1 us (13%)
  other arithmetic  8.12 us (10%)
  local copies, waits for them, and re-layouts  7.49 us (10%)
  waiting for transfers between devices  6.3 us (8%)
  between operations  0.93 us (1%)
    all_to_all x1, blocking collectives, body(): return lax.all_to_all(result, 'mp', split_axis=3, concat_axis=1, tiled=True)  22.1 us
    unnamed x1, other arithmetic  5.77 us
    all_to_all x1, starting transfers between devices, body(): lax.all_to_all(picked, 'dp', split_axis=0, concat_axis=1, tiled=True)  5.2 us
    dot_general x1, matrix products, newton_factors(): jnp.dot(square_one, product_one, preferred_element_type=jnp.float32)  5.06 us
    all_to_all x1, starting transfers between devices, body(): lax.all_to_all(gradient, 'mp', split_axis=1, concat_axis=3, tiled=True)  4.87 us
    unnamed x10, local copies, waits for them, and re-layouts  4 us
    all_to_all x1, waiting for transfers between devices, body(): lax.all_to_all(gradient, 'mp', split_axis=1, concat_axis=3, tiled=True)  3.85 us
    dot_general x1, matrix products, body(): jnp.einsum('ij,nkjc->nkic', stacked[2], lax.all_to_all(gradient, 'mp', sp...  3.71 us
  transfers between devices with their start and end apart: 2, of which 2 were waited for; matrix products, arithmetic and copies ran while one was open for 23% of the time, Pallas kernels for 0%

commit v1 on v0

v1 whole, which is shorter than its diff:
```python
import functools

import jax
import jax.numpy as jnp
from jax import lax
from jax.experimental import pallas as pl
from jax.experimental.pallas import tpu as pltpu
from jax.sharding import PartitionSpec as P

F32 = jnp.float32
BF16 = jnp.bfloat16
VMEM = pl.BlockSpec(memory_space=pltpu.VMEM)
SMEM = pl.BlockSpec(memory_space=pltpu.SMEM)


def dot(a, b):
    return jnp.dot(a, b, preferred_element_type=F32)


def pick_kernel(assignment, rows, out):
    for owner in range(out.shape[0]):
        out[owner] = rows[assignment[0, owner]].astype(out.dtype)


def pick(factor_rows, assignment):
    blocks, rows, width = factor_rows.shape
    return pl.pallas_call(
        pick_kernel,
        out_shape=jax.ShapeDtypeStruct((blocks, rows, width), F32),
        in_specs=[SMEM, VMEM],
        out_specs=VMEM,
        name="pick",
    )(assignment, factor_rows)


def newton_kernel(block, rows_ref, old, s1, s2, s3, stat, normed, square, product, coupled):
    order = old.shape[0]
    rows = rows_ref[...].reshape(rows_ref.shape[0], order).astype(BF16)
    strips = [slice(start, start + block) for start in range(0, order, block)]

    def five_eye(strip):
        shape = (block, order)
        row = lax.broadcasted_iota(jnp.int32, shape, 0) + strip.start
        column = lax.broadcasted_iota(jnp.int32, shape, 1)
        return jnp.where(row == column, F32(5.0), F32(0.0))

    total = jnp.zeros((1, order), F32)
    for strip in strips:
        gram = lax.dot_general(
            rows[:, strip], rows, (((0,), (0,)), ((), ())), preferred_element_type=F32
        )
        value = old[strip, :] + gram / rows.shape[0]
        stat[strip, :] = value
        total = total + jnp.sum(value * value, axis=0, keepdims=True)
    frob = jnp.sqrt(jnp.sum(total, axis=1, keepdims=True) + F32(1e-06))
    inverse = 1.0 / frob
    for strip in strips:
        value = stat[strip, :] * inverse
        normed[strip, :] = value.astype(BF16)
        s1[strip, :] = ((five_eye(strip) - value) * 0.25).astype(BF16)

    def multiply(step, state):
        for strip in strips:
            square[strip, :] = dot(step[strip, :], step[...]).astype(BF16)
        for strip in strips:
            product[strip, :] = dot(square[strip, :], state[...]).astype(BF16)

    multiply(s1, normed)
    for strip in strips:
        value = dot(square[strip, :], product[...])
        coupled[strip, :] = value.astype(BF16)
        s2[strip, :] = ((five_eye(strip) - value) * 0.25).astype(BF16)
    multiply(s2, coupled)
    scale = 1.0 / (4.0 * jnp.sqrt(jnp.sqrt(frob)))
    for strip in strips:
        value = dot(square[strip, :], product[...])
        s3[strip, :] = ((five_eye(strip) - value) * scale).astype(BF16)


def newton(rows, old):
    order = old.shape[-1]
    block = 256 if order % 256 == 0 else order
    factor = jax.ShapeDtypeStruct((order, order), BF16)
    return pl.pallas_call(
        functools.partial(newton_kernel, block),
        out_shape=[factor] * 3,
        in_specs=[VMEM, VMEM],
        out_specs=[VMEM] * 3,
        scratch_shapes=[pltpu.VMEM((order, order), F32)] + [pltpu.VMEM((order, order), BF16)] * 4,
        compiler_params=pltpu.CompilerParams(vmem_limit_bytes=24 << 20),
        cost_estimate=pl.CostEstimate(
            flops=12 * order**3, bytes_accessed=10 * order * order, transcendentals=0
        ),
        name="newton",
    )(rows, old)


def apply_kernel(s1, s2, s3, *refs):
    half = len(refs) // 2
    value = jnp.concatenate([ref[...] for ref in refs[:half]], axis=1)
    for step in (s3, s2, s1):
        value = dot(step[...], value).astype(BF16)
    width = value.shape[1] // half
    for index in range(half):
        refs[half + index][...] = value[:, index * width : (index + 1) * width]


def apply(factors, *blocks):
    order, width = blocks[0].shape
    return pl.pallas_call(
        apply_kernel,
        out_shape=[jax.ShapeDtypeStruct((order, width), BF16)] * len(blocks),
        in_specs=[VMEM] * (3 + len(blocks)),
        out_specs=[VMEM] * len(blocks),
        compiler_params=pltpu.CompilerParams(vmem_limit_bytes=16 << 20),
        cost_estimate=pl.CostEstimate(
            flops=6 * order * order * width * len(blocks),
            bytes_accessed=6 * order * order,
            transcendentals=0,
        ),
        name="apply",
    )(*factors, *blocks)


def solution(mesh):
    n_mp = mesh.shape["mp"]

    def exchange(block, flip):
        return lax.ppermute(block, "mp", [(i, i ^ flip) for i in range(n_mp)])

    def body(factor_rows, old_statistic, assignment, gradient):
        me = lax.axis_index("mp")
        blocks = gradient[0]

        def mine(flip):
            return lax.dynamic_index_in_dim(blocks, me ^ flip, 0, keepdims=False)

        picked = pick(factor_rows[0], assignment)
        arrived = lax.all_to_all(picked, "dp", split_axis=0, concat_axis=0, tiled=True)
        rows = arrived.reshape(-1, arrived.shape[-1])
        flips = list(range(n_mp - 1, 0, -1))
        came = {flip: exchange(mine(flip), flip) for flip in flips}
        factors = newton(rows, old_statistic[0, 0])
        own, first = apply(factors, mine(0), came[flips[0]])
        done = {0: own, flips[0]: exchange(first, flips[0])}
        for flip in flips[1:]:
            done[flip] = exchange(apply(factors, came[flip])[0], flip)
        result = jnp.zeros_like(blocks)
        for flip, value in done.items():
            result = lax.dynamic_update_index_in_dim(result, value, me ^ flip, 0)
        return result[None]

    return jax.shard_map(
        body,
        mesh=mesh,
        in_specs=(
            P("mp", None, "dp", None),
            P("dp", "mp", None, None),
            P("mp", None),
            P("dp", None, None, "mp"),
        ),
        out_specs=P("dp", None, None, "mp"),
        check_vma=False,
    )
```

time: 77.8 us -> 51.5 us (0.66)
  matrix products: 22.3 us -> 0 us
  blocking collectives: 22.1 us -> 0 us
  waiting for transfers between devices: 6.3 us -> 18.2 us
  Pallas kernels: 0 us -> 11.5 us
  other arithmetic: 8.12 us -> 0 us
  starting transfers between devices: 10.1 us -> 14.6 us
  between operations: 0.93 us -> 0.07 us
    dot_general x7 -> x0, matrix products: 22.3 us -> none  [the longest x1 5.06 us: newton_factors(): jnp.dot(square_one, product_one, preferred_element_type=jnp.float32)]
    all_to_all x1 -> x0, blocking collectives: 22.1 us -> none  [body(): return lax.all_to_all(result, 'mp', split_axis=3, concat_axis=1, tiled=True)]
    ppermute x0 -> x6, waiting for transfers between devices: none -> 18.2 us  [exchange(): return lax.ppermute(block, 'mp', [(i, i ^ flip) for i in range(n_mp)])]
    pallas_call x0 -> x4, Pallas kernels: none -> 11.5 us  [the longest x1 6.79 us: newton(): pl.pallas_call(functools.partial(newton_kernel, block), out_shape=[factor...]
    ppermute x0 -> x6, starting transfers between devices: none -> 9.37 us  [exchange(): return lax.ppermute(block, 'mp', [(i, i ^ flip) for i in range(n_mp)])]
    all_to_all x2 -> x1, waiting for transfers between devices: 6.3 us -> 0.01 us  [body(): lax.all_to_all(picked, 'dp', split_axis=0, concat_axis=0, tiled=True)]
    unnamed x1 -> x0, other arithmetic: 5.77 us -> none
    all_to_all x2 -> x1, starting transfers between devices: 10.1 us -> 5.2 us  [body(): lax.all_to_all(picked, 'dp', split_axis=0, concat_axis=0, tiled=True)]
  transfers between devices with their start and end apart: 2 -> 7, of which waited for: 2 -> 4; matrix products, arithmetic and copies ran while one was open for 23% -> 6% of each run, Pallas kernels for 0% -> 20%
where the time goes in v1:
time: 51.5 us; the launch traced here: 51.2 us
  waiting for transfers between devices  18.2 us (35%)
  starting transfers between devices  14.6 us (28%)
  Pallas kernels  11.5 us (22%)
  local copies, waits for them, and re-layouts  6.88 us (13%)
    ppermute x6, waiting for transfers between devices, exchange(): return lax.ppermute(block, 'mp', [(i, i ^ flip) for i in range(n_mp)])  18.2 us
    ppermute x6, starting transfers between devices, exchange(): return lax.ppermute(block, 'mp', [(i, i ^ flip) for i in range(n_mp)])  9.37 us
    pallas_call x1, Pallas kernels, newton(): pl.pallas_call(functools.partial(newton_kernel, block), out_shape=[factor...  6.79 us
    all_to_all x1, starting transfers between devices, body(): lax.all_to_all(picked, 'dp', split_axis=0, concat_axis=0, tiled=True)  5.2 us
    pallas_call x2, Pallas kernels, apply(): pl.pallas_call(apply_kernel, out_shape=[jax.ShapeDtypeStruct((order, widt...  3.34 us
    pallas_call x1, local copies, waits for them, and re-layouts, apply(): pl.pallas_call(apply_kernel, out_shape=[jax.ShapeDtypeStruct((order, widt...  1.76 us
    unnamed x5, local copies, waits for them, and re-layouts  1.67 us
    pallas_call x1, Pallas kernels, pick(): pl.pallas_call(pick_kernel, out_shape=jax.ShapeDtypeStruct((blocks, rows,...  1.36 us
  transfers between devices with their start and end apart: 7, of which 4 were waited for; matrix products, arithmetic and copies ran while one was open for 6% of the time, Pallas kernels for 20%

profile of v1, /device:TPU:0, one launch (start us, length us, event | category | flops | bytes accessed | tf_op | source)
XLA Modules:
  0.0 51.2 jit_solution(16239457030986831455)
XLA Ops:
  0.0 1.3 %copy.8.rows = bf16[8,1,768]{2,1,0:T(2,128)(2,1)} copy(bf16[8,1,768]{2,0,1:T(8,128)(2,1)} %bitcast.23) | data formatting | bytes 24576 | tf_op jit(solution)/shard_map/squeeze | solution.py:138
  1.3 1.4 %pick.1 = f32[8,1,768]{2,1,0:T(1,128)} custom-call(s32[1,8]{1,0:T(1,128)} %assignment.1, bf16[8,1,768]{2,1,0:T(2,128)(2,1)} %copy.8.rows), custom_call_target="tpu_custom_call" | custom-call | tf_op jit(solution)/shard_map/pick/pallas_call | solution.py:27
  2.7 5.2 %all-to-all-start = ((f32[8,1,768]{2,1,0:T(1,128)}), f32[8,1,768]{2,1,0:T(1,128)S(1)}, u32[]{:S(2)}, u32[]{:S(2)}) async-start(f32[8,1,768]{2,1,0:T(1,128)} %pick.1), calls=%async_computation | async-start | bytes 49152 | tf_op jit(solution)/shard_map/all_to_all | solution.py:139
  7.9 1.3 %dynamic-slice_bitcast_fusion = (bf16[768,128]{1,0:T(8,128)(2,1)S(1)}, bf16[768,128]{1,0:T(8,128)(2,1)S(1)}, bf16[768,128]{1,0:T(8,128)(2,1)S(1)}, bf16[768,128]{1,0:T(8,128)(2,1)S(1)}) fusion(bf16[1,4,768,128]{3,2,1,0:T(8,128)(2,1)} %param.7, s32[]{:T(128)S(6)} %select_n.21, s32[]{:T(128)S(6)} %select_n.19, s32[]{:T(128)S(6)} %select_n.18, s32[]{:T(128)S(6)} %select_n.20), kind=kLoop, calls=%fused_computation.4 | loop fusion | bytes 1572880 | tf_op jit(solution)/shard_map/jit(dynamic_index_in_dim)/squeeze | solution.py:136
  9.2 1.6 %collective-permute-start.4 = (bf16[768,128]{1,0:T(8,128)(2,1)S(1)}, bf16[768,128]{1,0:T(8,128)(2,1)S(1)}, u32[]{:S(2)}, u32[]{:S(2)}) collective-permute-start(bf16[768,128]{1,0:T(8,128)(2,1)S(1)} %get-tuple-element.19), channel_id=1, source_target_pairs={{0,1},{1,0},{2,3},{3,2},{4,5},{5,4},{6,7},{7,6},{8,9},{9,8},{10,11... | collective-permute-start | bytes 589832 | tf_op jit(solution)/shard_map/ppermute | solution.py:129
  10.8 2.5 %collective-permute-start = (bf16[768,128]{1,0:T(8,128)(2,1)S(1)}, bf16[768,128]{1,0:T(8,128)(2,1)S(1)}, u32[]{:S(2)}, u32[]{:S(2)}) collective-permute-start(bf16[768,128]{1,0:T(8,128)(2,1)S(1)} %get-tuple-element.20), channel_id=1, source_target_pairs={{0,3},{1,2},{2,1},{3,0},{4,7},{5,6},{6,5},{7,4},{8,11},{9,10},{10,... | collective-permute-start | bytes 589832 | tf_op jit(solution)/shard_map/ppermute | solution.py:129
  13.3 0.1 collective-permute-start.2
  13.4 0.0 all-to-all-done
  13.4 0.0 copy-start
  13.4 1.7 %copy-done = f32[1,1,768,768]{3,2,1,0:T(8,128)S(1)} copy-done((f32[1,1,768,768]{3,2,1,0:T(8,128)S(1)}, f32[1,1,768,768]{3,2,1,0:T(8,128)}, u32[]{:S(2)}) %copy-start) | copy-done | bytes 2359320
  15.1 6.8 %newton.1 = (bf16[768,768]{1,0:T(8,128)(2,1)S(1)}, bf16[768,768]{1,0:T(8,128)(2,1)S(1)}, bf16[768,768]{1,0:T(8,128)(2,1)S(1)}) custom-call(f32[8,768]{1,0:T(8,128)S(1)} %bitcast.21, f32[768,768]{1,0:T(8,128)S(1)} %bitcast.22), custom_call_target="tpu_custom_call" | custom-call | flops 5435817984 | bytes 5898240 | tf_op jit(solution)/shard_map/newton/pallas_call | solution.py:84
  21.9 1.5 %collective-permute-done = bf16[768,128]{1,0:T(8,128)(2,1)S(1)} collective-permute-done((bf16[768,128]{1,0:T(8,128)(2,1)S(1)}, bf16[768,128]{1,0:T(8,128)(2,1)S(1)}, u32[]{:S(2)}, u32[]{:S(2)}) %collective-permute-start) | collective-permute-done | bytes 196640 | tf_op jit(solution)/shard_map/ppermute | solution.py:129
  23.3 0.1 broadcast_in_dim.17
  23.4 1.8 %apply.5 = (bf16[1,4,768,128]{3,2,1,0:T(8,128)(2,1)S(1)}, bf16[768,128]{1,0:T(8,128)(2,1)S(1)}) fusion(bf16[1,4,768,128]{3,2,1,0:T(8,128)(2,1)S(1)} %broadcast_in_dim.17, s32[]{:T(128)S(6)} %select_n.18, bf16[768,768]{1,0:T(8,128)(2,1)S(1)} %get-tuple-element.10.s1, bf16[768,768]{1,0:T(8,128)(2,1)S(1)} %get-tuple-element.11.s2, ...), kind=kCustom, calls=%fused_computation.3 | custom fusion | bytes 4325380 | tf_op jit(solution)/shard_map/apply/pallas_call | solution.py:110
  25.2 1.5 %collective-permute-start.1 = (bf16[768,128]{1,0:T(8,128)(2,1)S(1)}, bf16[768,128]{1,0:T(8,128)(2,1)S(1)}, u32[]{:S(2)}, u32[]{:S(2)}) collective-permute-start(bf16[768,128]{1,0:T(8,128)(2,1)S(1)} %get-tuple-element.18), channel_id=1, source_target_pairs={{0,3},{1,2},{2,1},{3,0},{4,7},{5,6},{6,5},{7,4},{8,11},{9,10},{10,... | collective-permute-start | bytes 589832 | tf_op jit(solution)/shard_map/ppermute | solution.py:129
  26.7 9.3 %collective-permute-done.2.refs_0_ = bf16[768,128]{1,0:T(8,128)(2,1)S(1)} collective-permute-done((bf16[768,128]{1,0:T(8,128)(2,1)S(1)}, bf16[768,128]{1,0:T(8,128)(2,1)S(1)}, u32[]{:S(2)}, u32[]{:S(2)}) %collective-permute-start.2) | collective-permute-done | bytes 196640 | tf_op jit(solution)/shard_map/ppermute | solution.py:129
  36.0 1.7 %apply.3 = bf16[768,128]{1,0:T(8,128)(2,1)S(1)} custom-call(bf16[768,768]{1,0:T(8,128)(2,1)S(1)} %get-tuple-element.10.s1, bf16[768,768]{1,0:T(8,128)(2,1)S(1)} %get-tuple-element.11.s2, bf16[768,768]{1,0:T(8,128)(2,1)S(1)} %get-tuple-element.12.s3, bf16[768,128]{1,0:T(8,128)(2,1)S(1)} %collective-permute-done.2.refs_0_), custom_call_target="tpu_custom_call" | custom-call | flops 452984832 | bytes 3538944 | tf_op jit(solution)/shard_map/apply/pallas_call | solution.py:110
  37.7 0.1 collective-permute-start.3
  37.8 0.0 collective-permute-done.4.refs_0_
  37.8 1.7 %apply.4 = bf16[768,128]{1,0:T(8,128)(2,1)S(1)} custom-call(bf16[768,768]{1,0:T(8,128)(2,1)S(1)} %get-tuple-element.10.s1, bf16[768,768]{1,0:T(8,128)(2,1)S(1)} %get-tuple-element.11.s2, bf16[768,768]{1,0:T(8,128)(2,1)S(1)} %get-tuple-element.12.s3, bf16[768,128]{1,0:T(8,128)(2,1)S(1)} %collective-permute-done.4.refs_0_), custom_call_target="tpu_custom_call" | custom-call | flops 452984832 | bytes 3538944 | tf_op jit(solution)/shard_map/apply/pallas_call | solution.py:110
  39.4 3.5 %collective-permute-start.5 = (bf16[768,128]{1,0:T(8,128)(2,1)S(1)}, bf16[768,128]{1,0:T(8,128)(2,1)S(1)}, u32[]{:S(2)}, u32[]{:S(2)}) collective-permute-start(bf16[768,128]{1,0:T(8,128)(2,1)S(1)} %apply.4), channel_id=1, source_target_pairs={{0,1},{1,0},{2,3},{3,2},{4,5},{5,4},{6,7},{7,6},{8,9},{9,8},{10,11... | collective-permute-start | bytes 589832 | tf_op jit(solution)/shard_map/ppermute | solution.py:129
  43.0 0.0 collective-permute-done.1
  43.0 5.7 %collective-permute-done.3 = bf16[768,128]{1,0:T(8,128)(2,1)S(1)} collective-permute-done((bf16[768,128]{1,0:T(8,128)(2,1)S(1)}, bf16[768,128]{1,0:T(8,128)(2,1)S(1)}, u32[]{:S(2)}, u32[]{:S(2)}) %collective-permute-start.3) | collective-permute-done | bytes 196640 | tf_op jit(solution)/shard_map/ppermute | solution.py:129
  48.7 0.0 copy-start.1
  48.7 1.8 %collective-permute-done.5 = bf16[768,128]{1,0:T(8,128)(2,1)S(1)} collective-permute-done((bf16[768,128]{1,0:T(8,128)(2,1)S(1)}, bf16[768,128]{1,0:T(8,128)(2,1)S(1)}, u32[]{:S(2)}, u32[]{:S(2)}) %collective-permute-start.5) | collective-permute-done | bytes 196640 | tf_op jit(solution)/shard_map/ppermute | solution.py:129
  50.5 0.0 copy-done.1
  50.5 0.7 %bitcast_dynamic-update-slice_fusion = bf16[1,4,768,128]{3,2,1,0:T(8,128)(2,1)} fusion(bf16[1,4,768,128]{3,2,1,0:T(8,128)(2,1)} %copy-done.1, s32[]{:T(128)S(6)} %select_n.21, bf16[768,128]{1,0:T(8,128)(2,1)S(1)} %collective-permute-done.5), kind=kLoop, calls=%fused_computation | loop fusion | bytes 393220 | tf_op jit(solution)/shard_map/jit(dynamic_update_index_in_dim)/dynamic_update_slice | solution.py:150
  (3 shorter events, 0.1 us)
Async XLA Ops:
  2.7 10.7 %all-to-all-start = ((f32[8,1,768]{2,1,0:T(1,128)}), f32[8,1,768]{2,1,0:T(1,128)S(1)}, u32[]{:S(2)}, u32[]{:S(2)}) async-start(f32[8,1,768]{2,1,0:T(1,128)} %pick.1), calls=%async_computation | async-start | bytes 49152 | tf_op jit(solution)/shard_map/all_to_all | solution.py:139
  9.2 28.6 %collective-permute-start.4 = (bf16[768,128]{1,0:T(8,128)(2,1)S(1)}, bf16[768,128]{1,0:T(8,128)(2,1)S(1)}, u32[]{:S(2)}, u32[]{:S(2)}) collective-permute-start(bf16[768,128]{1,0:T(8,128)(2,1)S(1)} %get-tuple-element.19), channel_id=1, source_target_pairs={{0,1},{1,0},{2,3},{3,2},{4,5},{5,4},{6,7},{7,6},{8,9},{9,8},{10,11... | collective-permute-start | bytes 589832 | tf_op jit(solution)/shard_map/ppermute | solution.py:129
  10.8 12.5 %collective-permute-start = (bf16[768,128]{1,0:T(8,128)(2,1)S(1)}, bf16[768,128]{1,0:T(8,128)(2,1)S(1)}, u32[]{:S(2)}, u32[]{:S(2)}) collective-permute-start(bf16[768,128]{1,0:T(8,128)(2,1)S(1)} %get-tuple-element.20), channel_id=1, source_target_pairs={{0,3},{1,2},{2,1},{3,0},{4,7},{5,6},{6,5},{7,4},{8,11},{9,10},{10,... | collective-permute-start | bytes 589832 | tf_op jit(solution)/shard_map/ppermute | solution.py:129
  13.3 22.7 %collective-permute-start.2 = (bf16[768,128]{1,0:T(8,128)(2,1)S(1)}, bf16[768,128]{1,0:T(8,128)(2,1)S(1)}, u32[]{:S(2)}, u32[]{:S(2)}) collective-permute-start(bf16[768,128]{1,0:T(8,128)(2,1)S(1)} %get-tuple-element.22), channel_id=1, source_target_pairs={{0,2},{1,3},{2,0},{3,1},{4,6},{5,7},{6,4},{7,5},{8,10},{9,11},{10,... | collective-permute-start | bytes 589832 | tf_op jit(solution)/shard_map/ppermute | solution.py:129
  13.4 1.7 %copy-start = (f32[1,1,768,768]{3,2,1,0:T(8,128)S(1)}, f32[1,1,768,768]{3,2,1,0:T(8,128)}, u32[]{:S(2)}) copy-start(f32[1,1,768,768]{3,2,1,0:T(8,128)} %param.5) | copy-start | bytes 7077892
  25.2 17.8 %collective-permute-start.1 = (bf16[768,128]{1,0:T(8,128)(2,1)S(1)}, bf16[768,128]{1,0:T(8,128)(2,1)S(1)}, u32[]{:S(2)}, u32[]{:S(2)}) collective-permute-start(bf16[768,128]{1,0:T(8,128)(2,1)S(1)} %get-tuple-element.18), channel_id=1, source_target_pairs={{0,3},{1,2},{2,1},{3,0},{4,7},{5,6},{6,5},{7,4},{8,11},{9,10},{10,... | collective-permute-start | bytes 589832 | tf_op jit(solution)/shard_map/ppermute | solution.py:129
  37.7 11.0 %collective-permute-start.3 = (bf16[768,128]{1,0:T(8,128)(2,1)S(1)}, bf16[768,128]{1,0:T(8,128)(2,1)S(1)}, u32[]{:S(2)}, u32[]{:S(2)}) collective-permute-start(bf16[768,128]{1,0:T(8,128)(2,1)S(1)} %apply.3), channel_id=1, source_target_pairs={{0,2},{1,3},{2,0},{3,1},{4,6},{5,7},{6,4},{7,5},{8,10},{9,11},{10,... | collective-permute-start | bytes 589832 | tf_op jit(solution)/shard_map/ppermute | solution.py:129
  39.4 11.1 %collective-permute-start.5 = (bf16[768,128]{1,0:T(8,128)(2,1)S(1)}, bf16[768,128]{1,0:T(8,128)(2,1)S(1)}, u32[]{:S(2)}, u32[]{:S(2)}) collective-permute-start(bf16[768,128]{1,0:T(8,128)(2,1)S(1)} %apply.4), channel_id=1, source_target_pairs={{0,1},{1,0},{2,3},{3,2},{4,5},{5,4},{6,7},{7,6},{8,9},{9,8},{10,11... | collective-permute-start | bytes 589832 | tf_op jit(solution)/shard_map/ppermute | solution.py:129
  48.7 1.8 %copy-start.1 = (bf16[1,4,768,128]{3,2,1,0:T(8,128)(2,1)}, bf16[1,4,768,128]{3,2,1,0:T(8,128)(2,1)S(1)}, u32[]{:S(2)}) copy-start(bf16[1,4,768,128]{3,2,1,0:T(8,128)(2,1)S(1)} %bitcast_dynamic-update-slice_fusion.1) | copy-start | bytes 2359300

commit v2 on v1

--- a/solution.py
+++ b/solution.py
@@ -7,35 +7,58 @@
 from jax.experimental.pallas import tpu as pltpu
 from jax.sharding import PartitionSpec as P
 
+
 F32 = jnp.float32
 BF16 = jnp.bfloat16
 VMEM = pl.BlockSpec(memory_space=pltpu.VMEM)
 SMEM = pl.BlockSpec(memory_space=pltpu.SMEM)
+HBM = pl.BlockSpec(memory_space=pltpu.HBM)
 
 
 def dot(a, b):
     return jnp.dot(a, b, preferred_element_type=F32)
 
 
-def pick_kernel(assignment, rows, out):
+def pick_kernel(assignment, rows, out, wide):
+    wide[...] = rows[...].astype(F32)
     for owner in range(out.shape[0]):
-        out[owner] = rows[assignment[0, owner]].astype(out.dtype)
+        out[owner] = wide[pl.ds(assignment[0, owner], 1), :]
 
 
 def pick(factor_rows, assignment):
-    blocks, rows, width = factor_rows.shape
+    blocks, width = factor_rows.shape
     return pl.pallas_call(
         pick_kernel,
-        out_shape=jax.ShapeDtypeStruct((blocks, rows, width), F32),
+        out_shape=jax.ShapeDtypeStruct((blocks, 1, width), F32),
         in_specs=[SMEM, VMEM],
         out_specs=VMEM,
+        scratch_shapes=[pltpu.VMEM((blocks, width), F32)],
+        compiler_params=pltpu.CompilerParams(vmem_limit_bytes=4 << 20),
         name="pick",
     )(assignment, factor_rows)
 
 
+def load_kernel(source, out, sem):
+    copy = pltpu.make_async_copy(source, out, sem)
+    copy.start()
+    copy.wait()
+
+
+def load(array):
+    return pl.pallas_call(
+        load_kernel,
+        out_shape=jax.ShapeDtypeStruct(array.shape, array.dtype),
+        in_specs=[HBM],
+        out_specs=VMEM,
+        scratch_shapes=[pltpu.SemaphoreType.DMA],
+        compiler_params=pltpu.CompilerParams(vmem_limit_bytes=8 << 20),
+        name="load",
+    )(array)
+
+
 def newton_kernel(block, rows_ref, old, s1, s2, s3, stat, normed, square, product, coupled):
     order = old.shape[0]
-    rows = rows_ref[...].reshape(rows_ref.shape[0], order).astype(BF16)
+    rows = rows_ref[...].astype(BF16)
     strips = [slice(start, start + block) for start in range(0, order, block)]
 
     def five_eye(strip):
@@ -124,6 +147,7 @@
 
 def solution(mesh):
     n_mp = mesh.shape["mp"]
+    flips = list(range(n_mp - 1, 0, -1))
 
     def exchange(block, flip):
         return lax.ppermute(block, "mp", [(i, i ^ flip) for i in range(n_mp)])
@@ -135,12 +159,12 @@
         def mine(flip):
             return lax.dynamic_index_in_dim(blocks, me ^ flip, 0, keepdims=False)
 
-        picked = pick(factor_rows[0], assignment)
+        came = {flip: exchange(mine(flip), flip) for flip in flips}
+        picked = pick(factor_rows[0, :, 0], assignment)
         arrived = lax.all_to_all(picked, "dp", split_axis=0, concat_axis=0, tiled=True)
         rows = arrived.reshape(-1, arrived.shape[-1])
-        flips = list(range(n_mp - 1, 0, -1))
-        came = {flip: exchange(mine(flip), flip) for flip in flips}
-        factors = newton(rows, old_statistic[0, 0])
+        old = load(old_statistic[0, 0])
+        factors = newton(rows, old)
         own, first = apply(factors, mine(0), came[flips[0]])
         done = {0: own, flips[0]: exchange(first, flips[0])}
         for flip in flips[1:]:

time: 51.5 us -> 51 us (level)
  waiting for transfers between devices: 18.2 us -> 16.5 us
  local copies, waits for them, and re-layouts: 6.88 us -> 8.34 us
    unnamed x5 -> x9, local copies, waits for them, and re-layouts: 1.67 us -> 3.77 us
    ppermute x6, waiting for transfers between devices: 18.2 us -> 16.5 us  [exchange(): return lax.ppermute(block, 'mp', [(i, i ^ flip) for i in range(n_mp)])]
    squeeze x1 -> x0, local copies, waits for them, and re-layouts: 1.33 us -> none  [body(): picked = pick(factor_rows[0], assignment)]
    squeeze x1, local copies, waits for them, and re-layouts: 1.27 us -> 1.95 us  [mine(): return lax.dynamic_index_in_dim(blocks, me ^ flip, 0, keepdims=False)]
    pallas_call x1 -> x2, Pallas kernels: 1.36 us -> 1.33 us  [the longest x1 1.16 us: pick(): pl.pallas_call(pick_kernel, out_shape=jax.ShapeDtypeStruct((blocks, 1, wi...]
  transfers between devices with their start and end apart: 7 -> 7, of which waited for: 4 -> 3; matrix products, arithmetic and copies ran while one was open for 6% -> 9% of each run, Pallas kernels for 20% -> 20%
where the time goes in v2:
time: 51 us; the launch traced here: 50.6 us
  waiting for transfers between devices  16.5 us (32%)
  starting transfers between devices  14.1 us (28%)
  Pallas kernels  11.5 us (23%)
  local copies, waits for them, and re-layouts  8.34 us (16%)
    ppermute x6, waiting for transfers between devices, exchange(): return lax.ppermute(block, 'mp', [(i, i ^ flip) for i in range(n_mp)])  16.5 us
    ppermute x6, starting transfers between devices, exchange(): return lax.ppermute(block, 'mp', [(i, i ^ flip) for i in range(n_mp)])  8.92 us
    pallas_call x1, Pallas kernels, newton(): pl.pallas_call(functools.partial(newton_kernel, block), out_shape=[factor...  6.86 us
    all_to_all x1, starting transfers between devices, body(): lax.all_to_all(picked, 'dp', split_axis=0, concat_axis=0, tiled=True)  5.2 us
    unnamed x9, local copies, waits for them, and re-layouts  3.77 us
    pallas_call x2, Pallas kernels, apply(): pl.pallas_call(apply_kernel, out_shape=[jax.ShapeDtypeStruct((order, widt...  3.34 us
    squeeze x1, local copies, waits for them, and re-layouts, mine(): return lax.dynamic_index_in_dim(blocks, me ^ flip, 0, keepdims=False)  1.95 us
    pallas_call x1, local copies, waits for them, and re-layouts, apply(): pl.pallas_call(apply_kernel, out_shape=[jax.ShapeDtypeStruct((order, widt...  1.76 us
  transfers between devices with their start and end apart: 7, of which 3 were waited for; matrix products, arithmetic and copies ran while one was open for 9% of the time, Pallas kernels for 20%

profile of v2, /device:TPU:0, one launch (start us, length us, event | category | flops | bytes accessed | tf_op | source)
XLA Modules:
  0.0 50.6 jit_solution(7004077472660384900)
XLA Ops:
  0.0 0.0 copy-start.1
  0.0 0.7 %copy-done.1 = bf16[1,8,1,768]{3,1,2,0:T(8,128)(2,1)S(1)} copy-done((bf16[1,8,1,768]{3,1,2,0:T(8,128)(2,1)S(1)}, bf16[1,8,1,768]{3,1,2,0:T(8,128)(2,1)}, u32[]{:S(2)}) %copy-start.1) | copy-done | bytes 12312
  0.7 0.0 copy-start.2
  0.7 0.7 %copy-done.2 = s32[1,8]{1,0:T(1,128)S(1)} copy-done((s32[1,8]{1,0:T(1,128)S(1)}, s32[1,8]{1,0:T(1,128)}, u32[]{:S(2)}) %copy-start.2) | copy-done | bytes 56
  1.4 1.2 %pick.1 = f32[8,1,768]{2,1,0:T(1,128)} custom-call(s32[1,8]{1,0:T(1,128)S(1)} %copy-done.2, bf16[8,768]{1,0:T(8,128)(2,1)S(1)} %bitcast.23), custom_call_target="tpu_custom_call" | custom-call | tf_op jit(solution)/shard_map/pick/pallas_call | solution.py:30
  2.5 5.2 %all-to-all-start = ((f32[8,1,768]{2,1,0:T(1,128)}), f32[8,1,768]{2,1,0:T(1,128)}, u32[]{:S(2)}, u32[]{:S(2)}) async-start(f32[8,1,768]{2,1,0:T(1,128)} %pick.1), calls=%async_computation | async-start | bytes 49152 | tf_op jit(solution)/shard_map/all_to_all | solution.py:164
  7.7 2.0 %dynamic-slice_bitcast_fusion = (bf16[768,128]{1,0:T(8,128)(2,1)S(1)}, bf16[768,128]{1,0:T(8,128)(2,1)}, bf16[768,128]{1,0:T(8,128)(2,1)S(1)}, bf16[768,128]{1,0:T(8,128)(2,1)S(1)}) fusion(bf16[1,4,768,128]{3,2,1,0:T(8,128)(2,1)} %param.7, s32[]{:T(128)S(6)} %select_n.21, s32[]{:T(128)S(6)} %select_n.19, s32[]{:T(128)S(6)} %select_n.18, s32[]{:T(128)S(6)} %select_n.20), kind=kLoop, calls=%fused_computation.4 | loop fusion | bytes 1572880 | tf_op jit(solution)/shard_map/jit(dynamic_index_in_dim)/squeeze | solution.py:160
  9.7 3.9 %collective-permute-start = (bf16[768,128]{1,0:T(8,128)(2,1)}, bf16[768,128]{1,0:T(8,128)(2,1)S(1)}, u32[]{:S(2)}, u32[]{:S(2)}) collective-permute-start(bf16[768,128]{1,0:T(8,128)(2,1)} %get-tuple-element.20), channel_id=1, source_target_pairs={{0,3},{1,2},{2,1},{3,0},{4,7},{5,6},{6,5},{7,4},{8,11},{9,10},{10,... | collective-permute-start | bytes 589832 | tf_op jit(solution)/shard_map/ppermute | solution.py:153
  13.5 0.0 collective-permute-start.2
  13.5 0.6 %collective-permute-start.4 = (bf16[768,128]{1,0:T(8,128)(2,1)S(1)}, bf16[768,128]{1,0:T(8,128)(2,1)S(1)}, u32[]{:S(2)}, u32[]{:S(2)}) collective-permute-start(bf16[768,128]{1,0:T(8,128)(2,1)S(1)} %get-tuple-element.19), channel_id=1, source_target_pairs={{0,1},{1,0},{2,3},{3,2},{4,5},{5,4},{6,7},{7,6},{8,9},{9,8},{10,11... | collective-permute-start | bytes 589832 | tf_op jit(solution)/shard_map/ppermute | solution.py:153
  14.1 0.0 copy-start
  14.1 1.7 %copy-done = f32[1,1,768,768]{3,2,1,0:T(8,128)S(1)} copy-done((f32[1,1,768,768]{3,2,1,0:T(8,128)S(1)}, f32[1,1,768,768]{3,2,1,0:T(8,128)}, u32[]{:S(2)}) %copy-start) | copy-done | bytes 2359320
  15.8 0.2 load.1.old
  15.9 0.0 all-to-all-done
  16.0 0.7 %copy.8 = f32[8,1,768]{2,0,1:T(8,128)S(1)} copy(f32[8,1,768]{2,1,0:T(1,128)} %all-to-all-done) | data formatting | bytes 49152
  16.7 6.9 %newton.1 = (bf16[768,768]{1,0:T(8,128)(2,1)S(1)}, bf16[768,768]{1,0:T(8,128)(2,1)S(1)}, bf16[768,768]{1,0:T(8,128)(2,1)S(1)}) custom-call(f32[8,768]{1,0:T(8,128)S(1)} %bitcast.22, f32[768,768]{1,0:T(8,128)S(1)} %load.1.old), custom_call_target="tpu_custom_call" | custom-call | flops 5435817984 | bytes 5898240 | tf_op jit(solution)/shard_map/newton/pallas_call | solution.py:107
  23.6 0.0 collective-permute-done
  23.6 0.1 broadcast_in_dim.17
  23.7 1.8 %apply.5 = (bf16[1,4,768,128]{3,2,1,0:T(8,128)(2,1)S(1)}, bf16[768,128]{1,0:T(8,128)(2,1)S(1)}) fusion(bf16[1,4,768,128]{3,2,1,0:T(8,128)(2,1)S(1)} %broadcast_in_dim.17, s32[]{:T(128)S(6)} %select_n.18, bf16[768,768]{1,0:T(8,128)(2,1)S(1)} %get-tuple-element.10.s1, bf16[768,768]{1,0:T(8,128)(2,1)S(1)} %get-tuple-element.11.s2, ...), kind=kCustom, calls=%fused_computation.3 | custom fusion | bytes 4325380 | tf_op jit(solution)/shard_map/apply/pallas_call | solution.py:133
  25.5 3.9 %collective-permute-start.1 = (bf16[768,128]{1,0:T(8,128)(2,1)S(1)}, bf16[768,128]{1,0:T(8,128)(2,1)S(1)}, u32[]{:S(2)}, u32[]{:S(2)}) collective-permute-start(bf16[768,128]{1,0:T(8,128)(2,1)S(1)} %get-tuple-element.18), channel_id=1, source_target_pairs={{0,3},{1,2},{2,1},{3,0},{4,7},{5,6},{6,5},{7,4},{8,11},{9,10},{10,... | collective-permute-start | bytes 589832 | tf_op jit(solution)/shard_map/ppermute | solution.py:153
  29.3 8.6 %collective-permute-done.2.refs_0_ = bf16[768,128]{1,0:T(8,128)(2,1)S(1)} collective-permute-done((bf16[768,128]{1,0:T(8,128)(2,1)S(1)}, bf16[768,128]{1,0:T(8,128)(2,1)S(1)}, u32[]{:S(2)}, u32[]{:S(2)}) %collective-permute-start.2) | collective-permute-done | bytes 196640 | tf_op jit(solution)/shard_map/ppermute | solution.py:153
  37.9 1.7 %apply.3 = bf16[768,128]{1,0:T(8,128)(2,1)S(1)} custom-call(bf16[768,768]{1,0:T(8,128)(2,1)S(1)} %get-tuple-element.10.s1, bf16[768,768]{1,0:T(8,128)(2,1)S(1)} %get-tuple-element.11.s2, bf16[768,768]{1,0:T(8,128)(2,1)S(1)} %get-tuple-element.12.s3, bf16[768,128]{1,0:T(8,128)(2,1)S(1)} %collective-permute-done.2.refs_0_), custom_call_target="tpu_custom_call" | custom-call | flops 452984832 | bytes 3538944 | tf_op jit(solution)/shard_map/apply/pallas_call | solution.py:133
  39.6 0.1 collective-permute-start.3
  39.6 0.0 collective-permute-done.4.refs_0_
  39.7 1.7 %apply.4 = bf16[768,128]{1,0:T(8,128)(2,1)S(1)} custom-call(bf16[768,768]{1,0:T(8,128)(2,1)S(1)} %get-tuple-element.10.s1, bf16[768,768]{1,0:T(8,128)(2,1)S(1)} %get-tuple-element.11.s2, bf16[768,768]{1,0:T(8,128)(2,1)S(1)} %get-tuple-element.12.s3, bf16[768,128]{1,0:T(8,128)(2,1)S(1)} %collective-permute-done.4.refs_0_), custom_call_target="tpu_custom_call" | custom-call | flops 452984832 | bytes 3538944 | tf_op jit(solution)/shard_map/apply/pallas_call | solution.py:133
  41.3 0.5 %collective-permute-start.5 = (bf16[768,128]{1,0:T(8,128)(2,1)S(1)}, bf16[768,128]{1,0:T(8,128)(2,1)S(1)}, u32[]{:S(2)}, u32[]{:S(2)}) collective-permute-start(bf16[768,128]{1,0:T(8,128)(2,1)S(1)} %apply.4), channel_id=1, source_target_pairs={{0,1},{1,0},{2,3},{3,2},{4,5},{5,4},{6,7},{7,6},{8,9},{9,8},{10,11... | collective-permute-start | bytes 589832 | tf_op jit(solution)/shard_map/ppermute | solution.py:153
  41.9 0.0 collective-permute-done.1
  41.9 6.0 %collective-permute-done.3 = bf16[768,128]{1,0:T(8,128)(2,1)S(1)} collective-permute-done((bf16[768,128]{1,0:T(8,128)(2,1)S(1)}, bf16[768,128]{1,0:T(8,128)(2,1)S(1)}, u32[]{:S(2)}, u32[]{:S(2)}) %collective-permute-start.3) | collective-permute-done | bytes 196640 | tf_op jit(solution)/shard_map/ppermute | solution.py:153
  47.9 0.0 copy-start.3
  47.9 2.0 %collective-permute-done.5 = bf16[768,128]{1,0:T(8,128)(2,1)S(1)} collective-permute-done((bf16[768,128]{1,0:T(8,128)(2,1)S(1)}, bf16[768,128]{1,0:T(8,128)(2,1)S(1)}, u32[]{:S(2)}, u32[]{:S(2)}) %collective-permute-start.5) | collective-permute-done | bytes 196640 | tf_op jit(solution)/shard_map/ppermute | solution.py:153
  49.9 0.0 copy-done.3
  49.9 0.7 %bitcast_dynamic-update-slice_fusion = bf16[1,4,768,128]{3,2,1,0:T(8,128)(2,1)} fusion(bf16[1,4,768,128]{3,2,1,0:T(8,128)(2,1)} %copy-done.3, s32[]{:T(128)S(6)} %select_n.21, bf16[768,128]{1,0:T(8,128)(2,1)S(1)} %collective-permute-done.5), kind=kLoop, calls=%fused_computation | loop fusion | bytes 393220 | tf_op jit(solution)/shard_map/jit(dynamic_update_index_in_dim)/dynamic_update_slice | solution.py:174
  (2 shorter events, 0.1 us)
Async XLA Ops:
  0.0 0.7 %copy-start.1 = (bf16[1,8,1,768]{3,1,2,0:T(8,128)(2,1)S(1)}, bf16[1,8,1,768]{3,1,2,0:T(8,128)(2,1)}, u32[]{:S(2)}) copy-start(bf16[1,8,1,768]{3,1,2,0:T(8,128)(2,1)} %param.4) | copy-start | bytes 36868
  0.7 0.7 %copy-start.2 = (s32[1,8]{1,0:T(1,128)S(1)}, s32[1,8]{1,0:T(1,128)}, u32[]{:S(2)}) copy-start(s32[1,8]{1,0:T(1,128)} %assignment.1) | copy-start | bytes 100
  2.5 13.4 %all-to-all-start = ((f32[8,1,768]{2,1,0:T(1,128)}), f32[8,1,768]{2,1,0:T(1,128)}, u32[]{:S(2)}, u32[]{:S(2)}) async-start(f32[8,1,768]{2,1,0:T(1,128)} %pick.1), calls=%async_computation | async-start | bytes 49152 | tf_op jit(solution)/shard_map/all_to_all | solution.py:164
  9.7 13.9 %collective-permute-start = (bf16[768,128]{1,0:T(8,128)(2,1)}, bf16[768,128]{1,0:T(8,128)(2,1)S(1)}, u32[]{:S(2)}, u32[]{:S(2)}) collective-permute-start(bf16[768,128]{1,0:T(8,128)(2,1)} %get-tuple-element.20), channel_id=1, source_target_pairs={{0,3},{1,2},{2,1},{3,0},{4,7},{5,6},{6,5},{7,4},{8,11},{9,10},{10,... | collective-permute-start | bytes 589832 | tf_op jit(solution)/shard_map/ppermute | solution.py:153
  13.5 24.4 %collective-permute-start.2 = (bf16[768,128]{1,0:T(8,128)(2,1)S(1)}, bf16[768,128]{1,0:T(8,128)(2,1)S(1)}, u32[]{:S(2)}, u32[]{:S(2)}) collective-permute-start(bf16[768,128]{1,0:T(8,128)(2,1)S(1)} %get-tuple-element.22), channel_id=1, source_target_pairs={{0,2},{1,3},{2,0},{3,1},{4,6},{5,7},{6,4},{7,5},{8,10},{9,11},{10,... | collective-permute-start | bytes 589832 | tf_op jit(solution)/shard_map/ppermute | solution.py:153
  13.5 26.1 %collective-permute-start.4 = (bf16[768,128]{1,0:T(8,128)(2,1)S(1)}, bf16[768,128]{1,0:T(8,128)(2,1)S(1)}, u32[]{:S(2)}, u32[]{:S(2)}) collective-permute-start(bf16[768,128]{1,0:T(8,128)(2,1)S(1)} %get-tuple-element.19), channel_id=1, source_target_pairs={{0,1},{1,0},{2,3},{3,2},{4,5},{5,4},{6,7},{7,6},{8,9},{9,8},{10,11... | collective-permute-start | bytes 589832 | tf_op jit(solution)/shard_map/ppermute | solution.py:153
  14.1 1.7 %copy-start = (f32[1,1,768,768]{3,2,1,0:T(8,128)S(1)}, f32[1,1,768,768]{3,2,1,0:T(8,128)}, u32[]{:S(2)}) copy-start(f32[1,1,768,768]{3,2,1,0:T(8,128)} %param.5) | copy-start | bytes 7077892
  25.5 16.4 %collective-permute-start.1 = (bf16[768,128]{1,0:T(8,128)(2,1)S(1)}, bf16[768,128]{1,0:T(8,128)(2,1)S(1)}, u32[]{:S(2)}, u32[]{:S(2)}) collective-permute-start(bf16[768,128]{1,0:T(8,128)(2,1)S(1)} %get-tuple-element.18), channel_id=1, source_target_pairs={{0,3},{1,2},{2,1},{3,0},{4,7},{5,6},{6,5},{7,4},{8,11},{9,10},{10,... | collective-permute-start | bytes 589832 | tf_op jit(solution)/shard_map/ppermute | solution.py:153
  39.6 8.3 %collective-permute-start.3 = (bf16[768,128]{1,0:T(8,128)(2,1)S(1)}, bf16[768,128]{1,0:T(8,128)(2,1)S(1)}, u32[]{:S(2)}, u32[]{:S(2)}) collective-permute-start(bf16[768,128]{1,0:T(8,128)(2,1)S(1)} %apply.3), channel_id=1, source_target_pairs={{0,2},{1,3},{2,0},{3,1},{4,6},{5,7},{6,4},{7,5},{8,10},{9,11},{10,... | collective-permute-start | bytes 589832 | tf_op jit(solution)/shard_map/ppermute | solution.py:153
  41.3 8.6 %collective-permute-start.5 = (bf16[768,128]{1,0:T(8,128)(2,1)S(1)}, bf16[768,128]{1,0:T(8,128)(2,1)S(1)}, u32[]{:S(2)}, u32[]{:S(2)}) collective-permute-start(bf16[768,128]{1,0:T(8,128)(2,1)S(1)} %apply.4), channel_id=1, source_target_pairs={{0,1},{1,0},{2,3},{3,2},{4,5},{5,4},{6,7},{7,6},{8,9},{9,8},{10,11... | collective-permute-start | bytes 589832 | tf_op jit(solution)/shard_map/ppermute | solution.py:153
  47.9 2.0 %copy-start.3 = (bf16[1,4,768,128]{3,2,1,0:T(8,128)(2,1)}, bf16[1,4,768,128]{3,2,1,0:T(8,128)(2,1)S(1)}, u32[]{:S(2)}) copy-start(bf16[1,4,768,128]{3,2,1,0:T(8,128)(2,1)S(1)} %bitcast_dynamic-update-slice_fusion.1) | copy-start | bytes 2359300
